TPU v7x, 512 devices: a whole 4x4x16 slice. The times are simulated.
512 devices in a mesh: stn: 64 (over x, z), tm: 8 (over y, core).
Axes of the slice: x: 4, y: 4, z: 16, core: 2. Of those that a mesh axis runs over, the one named last changes fastest.
Arguments:
- right_sides: bfloat16 [2048, 131072], P('tm', 'stn'), may hold values from -6 to 6
- factor_cols: bfloat16 [131072, 512], P('stn'), may hold values from -0.25 to 0.25
- diag_inverses: float32 [2, 256, 256], replicated, as said below
- panel_block: int32 [1], replicated, may hold values from 0 to 510
- decay_rate: float32 [131072], P('stn'), may hold values from 0.00048828125 to 0.1
- gaps: int32 [2048], replicated, may hold values 0 or 1
Outputs:
- filtered: bfloat16 [2048, 131072], P('tm', 'stn')
Inputs may be any that keep to these rules, and one draw needn't show every extreme that they name: `diag_inverses`: each block is lower triangular with diagonal entries between 1 and 2. The two panels are rows 256 * panel_block to 256 * panel_block + 2 * 256 - 1.
All inputs are finite; a program needn't handle non-finite values.
Results may differ from a plain program's by a relative error of at most 0.001.
Values may be sent and summed in bfloat16 or wider, within the bound.
A program may use at most 64 MiB of HBM per device.

v0:
```python
import jax
import jax.numpy as jnp
from jax import lax
from jax.sharding import PartitionSpec as P


def broadcast(block, axis, source):
    block = jnp.where(lax.axis_index(axis) == source, block, jnp.zeros_like(block))
    return lax.psum(block, axis)


def compose(earlier, later):
    new_aa = later[0] * earlier[0] + later[1] * earlier[2]
    new_ab = later[0] * earlier[1] + later[1] * earlier[3]
    new_ba = later[2] * earlier[0] + later[3] * earlier[2]
    new_bb = later[2] * earlier[1] + later[3] * earlier[3]
    new_lv = later[0] * earlier[4] + later[1] * earlier[5] + later[4]
    new_sl = later[2] * earlier[4] + later[3] * earlier[5] + later[5]
    return (new_aa, new_ab, new_ba, new_bb, new_lv, new_sl)


def block_prefix(inputs, gap_flags, rate):
    decay = jnp.exp(-rate)
    gain = 2.0 * rate * jnp.sqrt(rate)
    factor = jnp.where(gap_flags == 1, 0.5, 1.0).astype(jnp.float32)[:, None]
    elements = (
        factor * (decay * (1.0 + rate)),
        factor * decay + 0.0 * inputs,
        factor * (-decay * rate * rate) + 0.0 * inputs,
        factor * (decay * (1.0 - rate)) + 0.0 * inputs,
        jnp.zeros_like(inputs),
        gain * inputs,
    )
    elements = (elements[0] + 0.0 * inputs,) + elements[1:]
    return lax.associative_scan(compose, elements, axis=0)


def solve_panel(block, inverse):
    return lax.dot_general(
        block,
        inverse,
        (((1,), (1,)), ((), ())),
        precision=lax.Precision.HIGHEST,
        preferred_element_type=jnp.float32,
    )


def trailing(work, solved, which, first_row, factor_cols, global_rows):
    panel_rows = solved.shape[1]
    below = (global_rows >= first_row + panel_rows).astype(jnp.float32)
    columns = (
        factor_cols[:, which * panel_rows : (which + 1) * panel_rows].astype(jnp.float32)
        * below[:, None]
    )
    return work - lax.dot_general(
        solved,
        columns,
        (((1,), (1,)), ((), ())),
        precision=lax.Precision.HIGHEST,
        preferred_element_type=jnp.float32,
    )


def place(work, solved, first_row, device_idx):
    stn_rows = work.shape[1]
    holder = first_row // stn_rows
    offset = first_row - holder * stn_rows
    placed = lax.dynamic_update_slice_in_dim(work, solved, offset, 1)
    return jnp.where(device_idx == holder, placed, work)


def panel_step(work, which, start_row, factor_cols, diag_inverses, global_rows, device_idx):
    panel_rows = diag_inverses.shape[1]
    stn_rows = work.shape[1]
    first_row = start_row + which * panel_rows
    holder = first_row // stn_rows
    offset = first_row - holder * stn_rows
    rhs_block = lax.dynamic_slice_in_dim(work, offset, panel_rows, 1)
    solved_here = solve_panel(rhs_block, diag_inverses[which])
    solved = broadcast(solved_here, "stn", holder)
    work = place(work, solved, first_row, device_idx)
    return trailing(work, solved, which, first_row, factor_cols, global_rows)


def on_device(right_sides, factor_cols, diag_inverses, panel_block, decay_rate, gaps):
    work = right_sides.astype(jnp.float32)
    time_rows, stn_rows = work.shape
    panel_rows = diag_inverses.shape[1]
    device_idx = lax.axis_index("stn")
    global_rows = device_idx * stn_rows + lax.iota(jnp.int32, stn_rows)
    start_row = panel_block[0] * panel_rows
    for which in range(2):
        work = panel_step(
            work, which, start_row, factor_cols, diag_inverses, global_rows, device_idx
        )
    time_idx = lax.axis_index("tm")
    groups = lax.axis_size("tm")
    narrow = stn_rows // groups
    series = lax.all_to_all(work, "tm", split_axis=1, concat_axis=0, tiled=True)
    rates = lax.dynamic_slice_in_dim(decay_rate, time_idx * narrow, narrow)
    series_blocks = series.reshape(groups, time_rows, narrow)
    gap_blocks = gaps.reshape(groups, time_rows)

    def advance(carried, element):
        inputs, gap_flags = element
        prefix = block_prefix(inputs, gap_flags, rates)
        level = prefix[0] * carried[0] + prefix[1] * carried[1] + prefix[4]
        slope = prefix[2] * carried[0] + prefix[3] * carried[1] + prefix[5]
        return ((level[-1], slope[-1]), level.astype(jnp.bfloat16))

    zeros_row = jnp.zeros((narrow,), jnp.float32)
    _, levels = lax.scan(advance, (zeros_row, zeros_row), (series_blocks, gap_blocks))
    levels = levels.reshape(groups * time_rows, narrow)
    return lax.all_to_all(levels, "tm", split_axis=0, concat_axis=1, tiled=True)


def solution(mesh):
    return jax.shard_map(
        on_device,
        mesh=mesh,
        in_specs=(P("tm", "stn"), P("stn", None), P(), P(), P("stn"), P()),
        out_specs=P("tm", "stn"),
        check_vma=False,
    )
```

profile of v0, /device:TPU:1, one launch (start us, length us, event | category | flops | bytes accessed | tf_op | source)
XLA Modules:
  0.0 694.7 jit_solution(8325721366704118853)
XLA Ops:
  7.2 2.1 convolution_select_fusion.1
  9.4 2.8 convert_element_type.29
  12.2 260.4 %all-reduce.100.cloned.1.call-done = f32[256,256]{1,0:T(8,128)} async-done(((f32[256,256]{1,0:T(8,128)}), f32[256,256]{1,0:T(8,128)}) %all-reduce.100.cloned.1.call-update) | async-done | bytes 262160 | tf_op jit(solution)/shard_map/psum | solution.py:9
  272.7 1.7 select_dynamic-update-slice_fusion.1
  274.4 4.1 convolution_subtract_fusion.1
  278.5 1.1 convolution_select_fusion
  279.7 261.0 %all-reduce.102.cloned.1.call-done = f32[256,256]{1,0:T(8,128)} async-done(((f32[256,256]{1,0:T(8,128)}), f32[256,256]{1,0:T(8,128)}) %all-reduce.102.cloned.1.call-update) | async-done | bytes 262160 | tf_op jit(solution)/shard_map/psum | solution.py:9
  540.7 3.4 convolution_subtract_fusion
  544.2 1.5 copy.12
  545.7 15.1 %all-to-all-start = ((f32[256,8,256]{2,0,1:T(8,128)}), f32[256,8,256]{2,0,1:T(8,128)}, u32[]{:S(2)}, u32[]{:S(2)}) async-start(f32[256,8,256]{2,0,1:T(8,128)} %bitcast.38), calls=%async_computation | async-start | bytes 4194304 | tf_op jit(solution)/shard_map/all_to_all | solution.py:99
  560.8 0.8 fusion.26
  561.6 25.5 %all-to-all-done = f32[256,8,256]{2,0,1:T(8,128)} async-done(((f32[256,8,256]{2,0,1:T(8,128)}), f32[256,8,256]{2,0,1:T(8,128)}, u32[]{:S(2)}, u32[]{:S(2)}) %all-to-all-start) | async-done | bytes 2097184 | tf_op jit(solution)/shard_map/all_to_all | solution.py:99
  587.1 80.3 %while.17 = (s32[]{:T(128)}, f32[256]{0:T(256)S(1)}, f32[256]{0:T(256)S(1)}, bf16[8,256,256]{2,1,0:T(8,128)(2,1)}, s32[8,256]{1,0:T(8,128)S(1)}, /*index=5*/f32[...) while((s32[]{:T(128)}, f32[256]{0:T(256)S(1)}, ...), condition=%wide.region_3.4_spmd, body=%wide.region_2.3_spmd.sunk | while | flops 4393474 | bytes 37127632 | solution.py:112
  587.1 1.1 multiply_add_fusion.88
  589.7 0.2 slice.2363
  596.2 0.8 bitcast_dynamic-update-slice_fusion.2
  597.1 1.1 multiply_add_fusion.88
  606.3 0.8 bitcast_dynamic-update-slice_fusion.2
  607.2 1.1 multiply_add_fusion.88
  616.3 0.8 bitcast_dynamic-update-slice_fusion.2
  617.2 1.1 multiply_add_fusion.88
  626.4 0.8 bitcast_dynamic-update-slice_fusion.2
  627.2 1.1 multiply_add_fusion.88
  636.4 0.8 bitcast_dynamic-update-slice_fusion.2
  637.3 1.1 multiply_add_fusion.88
  646.4 0.8 bitcast_dynamic-update-slice_fusion.2
  647.3 1.1 multiply_add_fusion.88
  656.5 0.8 bitcast_dynamic-update-slice_fusion.2
  657.4 1.1 multiply_add_fusion.88
  666.5 0.8 bitcast_dynamic-update-slice_fusion.2
  667.3 19.4 %all_to_all.32 = bf16[8,256,256]{2,1,0:T(8,128)(2,1)S(1)} all-to-all(bf16[8,256,256]{2,1,0:T(8,128)(2,1)} %get-tuple-element.142), channel_id=1, replica_groups=mesh['stn'=64,'tm'=8] {'tm'}, dimensions={0} | all-to-all | bytes 2097152 | tf_op jit(solution)/shard_map/all_to_all | solution.py:114
  686.7 1.1 copy.10
  (2743 shorter events, 50.0 us)
Async XLA Ops:
  6.5 266.1 %all-reduce.100.cloned.1.call-start = ((), (), s32[]{:S(2)}) async-start(), calls=%async_computation.2 | async-start | bytes 524288 | tf_op jit(solution)/shard_map/psum | solution.py:9
  9.3 531.4 %all-reduce.102.cloned.1.call-start = ((), (), s32[]{:S(2)}) async-start(), calls=%async_computation.3 | async-start | bytes 524288 | tf_op jit(solution)/shard_map/psum | solution.py:9
  274.4 4.1 copy-start
  545.7 15.1 %copy-start.1 = (s32[2048]{0:T(1024)S(1)}, s32[2048]{0:T(1024)}, u32[]{:S(2)}) copy-start(s32[2048]{0:T(1024)} %param.13) | copy-start | bytes 24580
  545.7 41.4 %all-to-all-start = ((f32[256,8,256]{2,0,1:T(8,128)}), f32[256,8,256]{2,0,1:T(8,128)}, u32[]{:S(2)}, u32[]{:S(2)}) async-start(f32[256,8,256]{2,0,1:T(8,128)} %bitcast.38), calls=%async_computation | async-start | bytes 4194304 | tf_op jit(solution)/shard_map/all_to_all | solution.py:99
Sparse Core Ops, SparseCore 0:
  10.8 261.8 all-reduce.99
  279.8 260.8 all-reduce.101
where the time goes:
time: 695 us
  waiting for transfers between devices  547 us (79%)
  local copies, waits for them, and re-layouts  42 us (6%)
  other arithmetic  31.4 us (5%)
  blocking collectives  19.4 us (3%)
  starting transfers between devices  15.1 us (2%)
  loops' own time  14.9 us (2%)
  between operations  14.2 us (2%)
  matrix products  10.7 us (2%)
    psum x2, waiting for transfers between devices, broadcast(): return lax.psum(block, axis)  521 us
    slice x1216, local copies, waits for them, and re-layouts, block_prefix(): return lax.associative_scan(compose, elements, axis=0)  29.4 us
    all_to_all x1, waiting for transfers between devices, on_device(): series = lax.all_to_all(work, 'tm', split_axis=1, concat_axis=0, tiled=True)  25.5 us
    all_to_all x1, blocking collectives, on_device(): return lax.all_to_all(levels, 'tm', split_axis=0, concat_axis=1, tiled=True)  19.4 us
    all_to_all x1, starting transfers between devices, on_device(): series = lax.all_to_all(work, 'tm', split_axis=1, concat_axis=0, tiled=True)  15.1 us
    another operation x1, loops' own time, on_device(): lax.scan(advance, (zeros_row, zeros_row), (series_blocks, gap_blocks))  14.9 us
  transfers between devices with their start and end apart: 3, of which 3 were waited for; matrix products, arithmetic and copies ran while one was open for 1% of the time, Pallas kernels for 0%

commit v1 on v0

v1 whole, which is shorter than its diff:
```python
import functools

import jax
import jax.numpy as jnp
from jax import lax
from jax.experimental import pallas as pl
from jax.experimental.pallas import tpu as pltpu
from jax.sharding import PartitionSpec as P

MESH = pl.DeviceIdType.MESH
BLK = 256
SEGS = 8
RING = 16
CHUNK = 16
F32 = jnp.float32
BF16 = jnp.bfloat16


def dot(a, b):
    return lax.dot_general(a, b, (((1,), (0,)), ((), ())), preferred_element_type=F32)


def dot_t(a, b):
    return lax.dot_general(a, b, (((1,), (1,)), ((), ())), preferred_element_type=F32)


def split3(a):
    high = a.astype(BF16)
    rest = a - high.astype(F32)
    mid = rest.astype(BF16)
    return high, mid, (rest - mid.astype(F32)).astype(BF16)


def pick_kernel(nx, pb_ref, r0_ref, r1_ref, f_ref, c_ref):
    core = lax.rem(lax.axis_index("tm"), 2)
    rows = BLK // nx
    frows = BLK // 4 // nx
    half = pl.multiple_of(core * (BLK // 2), BLK // 2)
    for q in range(nx):
        c_ref[q, 0:rows, 0:BLK] = r0_ref[rows * q : rows * (q + 1), :]
        c_ref[q, 0:rows, BLK : 2 * BLK] = r1_ref[rows * q : rows * (q + 1), :]
        for side in range(2):
            c_ref[q, rows : rows + frows, BLK * side : BLK * (side + 1)] = f_ref[
                pl.ds(half + side * (BLK // 4) + frows * q, frows), :
            ]


def pick(right_sides, factor_cols, panel_block, nx):
    blocks = right_sides.shape[1] // BLK
    piece = BLK // nx + BLK // 4 // nx
    return pl.pallas_call(
        functools.partial(pick_kernel, nx),
        out_shape=jax.ShapeDtypeStruct((nx, piece, 2 * BLK), BF16),
        grid_spec=pltpu.PrefetchScalarGridSpec(
            num_scalar_prefetch=1,
            grid=(1,),
            in_specs=[
                pl.BlockSpec((BLK, BLK), lambda i, pb: (0, lax.rem(pb[0], blocks))),
                pl.BlockSpec((BLK, BLK), lambda i, pb: (0, lax.rem(pb[0] + 1, blocks))),
                pl.BlockSpec((BLK, BLK), lambda i, pb: (lax.rem(pb[0] + 1, blocks), 0)),
            ],
            out_specs=pl.BlockSpec((nx, piece, 2 * BLK), lambda i, pb: (0, 0, 0)),
        ),
        name="pick",
    )(panel_block, right_sides, right_sides, factor_cols)


def spread_kernel(
    nx, nz, blocks, pb_ref, c_ref, p_ref, f_ref,
    xs, zs, pan, fb, own_sem, xsend, xrecv, zsend, zrecv, psend, precv, fsend, frecv,
):
    me, tm = lax.axis_index("stn"), lax.axis_index("tm")
    x, z = me // nz, lax.rem(me, nz)
    core = lax.rem(tm, 2)
    other = tm + 1 - 2 * core
    piece = c_ref.shape[1]
    rows = BLK // nx
    chunks = piece // CHUNK
    half = nz // 2
    split = (chunks + 1) // 2
    right = x * nz + lax.rem(z + 1, nz)
    left = x * nz + lax.rem(z + nz - 1, nz)

    def along_x(d):
        return lax.rem(x + d, nx) * nz + z

    barrier = pltpu.get_barrier_semaphore()
    for where in [{"stn": right}, {"stn": left}] + [
        {"stn": along_x(d), "tm": other if flip else tm}
        for flip in range(2)
        for d in range(nx)
        if flip or d
    ]:
        pl.semaphore_signal(barrier, inc=1, device_id=where, device_id_type=MESH)
    pl.semaphore_wait(barrier, 2 + 2 * nx - 1)

    own = pltpu.make_async_copy(c_ref.at[x], xs.at[0], own_sem)
    own.start()
    sends = []
    for d in range(1, nx):
        copy = pltpu.make_async_remote_copy(
            src_ref=c_ref.at[lax.rem(x + d, nx)],
            dst_ref=xs.at[d],
            send_sem=xsend.at[d],
            recv_sem=xrecv.at[d],
            device_id={"stn": along_x(d)},
            device_id_type=MESH,
        )
        copy.start()
        sends.append(copy)
    own.wait()
    for copy in sends:
        copy.wait()

    block = pb_ref[0]
    holder0 = block // blocks
    holder1 = (block + 1) // blocks
    from0 = lax.rem(x - holder0 // nz + nx, nx)
    from1 = lax.rem(x - holder1 // nz + nx, nx)
    zs[0, :, 0:BLK] = xs[from1, :, 0:BLK]
    zs[0, :, BLK : 2 * BLK] = xs[from1, :, BLK : 2 * BLK]
    zs[0, 0:rows, 0:BLK] = xs[from0, 0:rows, 0:BLK]

    def hop(way, step, c):
        src = step if way == 0 else lax.rem(nz - step, nz)
        dst = step + 1 if way == 0 else nz - 1 - step
        return pltpu.make_async_remote_copy(
            src_ref=zs.at[src, pl.ds(c * CHUNK, CHUNK), :],
            dst_ref=zs.at[dst, pl.ds(c * CHUNK, CHUNK), :],
            send_sem=zsend.at[way, step, c],
            recv_sem=zrecv.at[way, step, c],
            device_id={"stn": right if way == 0 else left},
            device_id_type=MESH,
        )

    def last(way):
        return range(split) if way == 0 else range(split, chunks)

    for c in range(chunks):
        for way in range(2):
            hop(way, 0, c).start()

    def middle(step, _):
        for c in range(chunks):
            for way in range(2):
                hop(way, step - 1, c).wait_recv()
                hop(way, step, c).start()
        return 0

    lax.fori_loop(1, half - 1, middle, 0)
    for c in range(chunks):
        for way in range(2):
            hop(way, half - 2, c).wait_recv()
            if c in last(way):
                hop(way, half - 1, c).start()
    for way in range(2):
        for c in last(way):
            hop(way, half - 1, c).wait_recv()

    back0 = lax.rem(z - lax.rem(holder0, nz) + nz, nz)
    back1 = lax.rem(z - lax.rem(holder1, nz) + nz, nz)
    mine = pl.ds(pl.multiple_of(x * rows, rows), rows)
    pan[mine, 0:BLK] = zs[back0, 0:rows, 0:BLK]
    pan[mine, BLK : 2 * BLK] = zs[back1, 0:rows, BLK : 2 * BLK]
    fb[core, x] = zs[back1, rows:piece, :]

    sends = []
    for d in range(1, nx):
        copy = pltpu.make_async_remote_copy(
            src_ref=pan.at[mine, :],
            dst_ref=pan.at[mine, :],
            send_sem=psend.at[d],
            recv_sem=precv.at[d],
            device_id={"stn": along_x(d)},
            device_id_type=MESH,
        )
        copy.start()
        sends.append(copy)
    for flip in range(2):
        for d in range(nx):
            if flip or d:
                copy = pltpu.make_async_remote_copy(
                    src_ref=fb.at[core, x],
                    dst_ref=fb.at[core, x],
                    send_sem=fsend.at[flip, d],
                    recv_sem=frecv.at[flip, d],
                    device_id={"stn": along_x(d), "tm": other if flip else tm},
                    device_id_type=MESH,
                )
                copy.start()
                sends.append(copy)

    def drain(step, _):
        for c in range(chunks):
            for way in range(2):
                hop(way, step, c).wait_send()
        return 0

    lax.fori_loop(0, half - 1, drain, 0)
    for way in range(2):
        for c in last(way):
            hop(way, half - 1, c).wait_send()
    for copy in sends:
        copy.wait()
    p_ref[...] = pan[...]
    for side in range(2):
        for q in range(nx):
            lines = fb.shape[2]
            start = side * lines * nx + q * lines
            f_ref[start : start + lines, :] = fb[side, q]


def spread(candidates, panel_block, nx, nz, blocks):
    piece = candidates.shape[1]
    chunks = piece // CHUNK
    frows = BLK // 4 // nx
    half = nz // 2
    vmem = pl.BlockSpec(memory_space=pltpu.VMEM)
    dma = pltpu.SemaphoreType.DMA
    return pl.pallas_call(
        functools.partial(spread_kernel, nx, nz, blocks),
        out_shape=(
            jax.ShapeDtypeStruct((BLK, 2 * BLK), BF16),
            jax.ShapeDtypeStruct((BLK // 2, 2 * BLK), BF16),
        ),
        in_specs=[pl.BlockSpec(memory_space=pltpu.SMEM), vmem],
        out_specs=(vmem, vmem),
        scratch_shapes=[
            pltpu.VMEM((nx, piece, 2 * BLK), BF16),
            pltpu.VMEM((nz, piece, 2 * BLK), BF16),
            pltpu.VMEM((BLK, 2 * BLK), BF16),
            pltpu.VMEM((2, nx, frows, 2 * BLK), BF16),
            dma,
            dma((nx,)),
            dma((nx,)),
            dma((2, half, chunks)),
            dma((2, half, chunks)),
            dma((nx,)),
            dma((nx,)),
            dma((2, nx)),
            dma((2, nx)),
        ],
        compiler_params=pltpu.CompilerParams(collective_id=0, has_side_effects=True),
        name="spread",
    )(panel_block, candidates)


def permutation(transposed):
    rows = lax.broadcasted_iota(jnp.int32, (BLK, BLK), 1 if transposed else 0)
    cols = lax.broadcasted_iota(jnp.int32, (BLK, BLK), 0 if transposed else 1)
    steps = BLK // SEGS
    hit = cols == steps * lax.rem(rows, SEGS) + lax.div(rows, SEGS)
    return jnp.where(hit, 1.0, 0.0).astype(F32)


def halvings(gaps_ref):
    return jnp.where(gaps_ref[...] == 1, 0.5, 1.0).astype(F32)


def own_halvings(halved_ref, perm):
    tm = lax.axis_index("tm")
    row = jnp.concatenate(
        [halved_ref[pl.ds(2 * tm, 1), :], halved_ref[pl.ds(2 * tm + 1, 1), :]], axis=1
    )
    return dot((perm * row).astype(BF16), jnp.ones((BLK, BLK), BF16))


def shifted(a, by):
    return pltpu.roll(a, by, axis=0)


def seg_product(sp_ref):
    total = sp_ref[0:SEGS, :]
    for k in range(1, BLK // SEGS):
        total = total * sp_ref[SEGS * k : SEGS * (k + 1), :]
    return total


def local_kernel(
    pb_ref, panel_ref, f10_ref, diag_ref, r_ref, fc_ref, rate_ref, gaps_ref,
    w_ref, yx_ref, zx_ref, st_ref,
    perm_ref, hl_ref, s_ref, halved_ref, sp_ref, q_ref,
):
    i = pl.program_id(0)

    @pl.when(i == 0)
    def _():
        perm = permutation(False)
        perm_ref[...] = perm.astype(BF16)
        halved_ref[...] = halvings(gaps_ref)
        sp_ref[...] = own_halvings(halved_ref, perm)
        q_ref[...] = seg_product(sp_ref)
        panel = dot(perm_ref[...], panel_ref[...])
        first = panel[:, 0:BLK].astype(BF16)
        second = panel[:, BLK : 2 * BLK]
        solved = sum(dot_t(first, part) for part in reversed(split3(diag_ref[0])))
        s_ref[0] = solved
        parts = split3(solved)
        hl_ref[0:BLK, 0:BLK] = parts[0]
        hl_ref[BLK : 2 * BLK, 0:BLK] = parts[1]
        quarter = BLK // 4
        for n in range(4):
            side, col = n // 2, n % 2
            f10 = f10_ref[
                side * quarter : (side + 1) * quarter, BLK * col : BLK * (col + 1)
            ]
            s_ref[1, :, quarter * n : quarter * (n + 1)] = sum(
                dot_t(part, f10) for part in reversed(parts)
            )
        solved = lax.dot_general(
            second - s_ref[1],
            diag_ref[1],
            (((1,), (1,)), ((), ())),
            precision=lax.Precision.HIGHEST,
            preferred_element_type=F32,
        )
        s_ref[1] = solved
        parts = split3(solved)
        hl_ref[0:BLK, BLK : 2 * BLK] = parts[0]
        hl_ref[BLK : 2 * BLK, BLK : 2 * BLK] = parts[1]

    rel = lax.axis_index("stn") * pl.num_programs(0) + i - pb_ref[0]
    raw = dot(perm_ref[...], r_ref[...])
    both = dot_t(hl_ref[...], fc_ref[...])
    lower = raw - (both[0:BLK] + both[BLK : 2 * BLK])
    w_ref[...] = jnp.where(
        rel >= 2, lower, jnp.where(rel == 1, s_ref[1], jnp.where(rel == 0, s_ref[0], raw))
    )

    rate = rate_ref[...]
    e = jnp.broadcast_to(jnp.exp(-rate), (SEGS, BLK))
    y = jnp.zeros((SEGS, BLK), F32)
    z = jnp.zeros((SEGS, BLK), F32)
    for k in range(BLK // SEGS):
        a = e * sp_ref[SEGS * k : SEGS * (k + 1), :]
        z = a * (z + y)
        y = a * y + w_ref[SEGS * k : SEGS * (k + 1), :]

    seg = lax.broadcasted_iota(jnp.int32, (SEGS, BLK), 0)
    window = q_ref[...]
    by, steps = 1, BLK // SEGS
    while by < SEGS:
        f = jnp.where(seg >= by, window * jnp.exp(-(float(steps) * rate)), 0.0)
        ys, zs = shifted(y, by), shifted(z, by)
        z = z + f * (zs + float(steps) * ys)
        y = y + f * ys
        window = window * shifted(window, by)
        by, steps = by * 2, steps * 2
    st_ref[0:1, :] = y[SEGS - 1 : SEGS, :]
    st_ref[1:2, :] = z[SEGS - 1 : SEGS, :]
    yx_ref[...] = jnp.where(seg >= 1, shifted(y, 1), 0.0)
    zx_ref[...] = jnp.where(seg >= 1, shifted(z, 1), 0.0)


def local(panel, f10, diag, right_sides, factor_cols, rates, gaps, panel_block):
    time_rows, stations = right_sides.shape
    tile = pl.BlockSpec((time_rows, BLK), lambda i: (0, i))
    line = pl.BlockSpec((SEGS, BLK), lambda i: (0, i))

    def whole(shape):
        return pl.BlockSpec(shape, lambda i: (0,) * len(shape))

    return pl.pallas_call(
        local_kernel,
        grid=(stations // BLK,),
        out_shape=(
            jax.ShapeDtypeStruct((time_rows, stations), F32),
            jax.ShapeDtypeStruct((SEGS, stations), F32),
            jax.ShapeDtypeStruct((SEGS, stations), F32),
            jax.ShapeDtypeStruct((2, stations), F32),
        ),
        in_specs=[
            pl.BlockSpec(memory_space=pltpu.SMEM),
            whole(panel.shape),
            whole(f10.shape),
            whole(diag.shape),
            tile,
            pl.BlockSpec((BLK, 2 * BLK), lambda i: (i, 0)),
            pl.BlockSpec((1, BLK), lambda i: (0, i)),
            whole(gaps.shape),
        ],
        out_specs=(tile, line, line, pl.BlockSpec((2, BLK), lambda i: (0, i))),
        scratch_shapes=[
            pltpu.VMEM((BLK, BLK), BF16),
            pltpu.VMEM((2 * BLK, 2 * BLK), BF16),
            pltpu.VMEM((2, BLK, BLK), F32),
            pltpu.VMEM(gaps.shape, F32),
            pltpu.VMEM((BLK, BLK), F32),
            pltpu.VMEM((SEGS, BLK), F32),
        ],
        name="local",
    )(panel_block, panel, f10, diag, right_sides, factor_cols, rates, gaps)


def states_kernel(nt, st_ref, all_ref, buf, own_sem, send, recv):
    tm = lax.axis_index("tm")
    barrier = pltpu.get_barrier_semaphore()
    for d in range(1, nt):
        pl.semaphore_signal(
            barrier, inc=1, device_id={"tm": lax.rem(tm + d, nt)}, device_id_type=MESH
        )
    pl.semaphore_wait(barrier, nt - 1)
    own = pltpu.make_async_copy(st_ref, buf.at[0], own_sem)
    own.start()
    copies = []
    for d in range(1, nt):
        copy = pltpu.make_async_remote_copy(
            src_ref=st_ref,
            dst_ref=buf.at[d],
            send_sem=send.at[d],
            recv_sem=recv.at[d],
            device_id={"tm": lax.rem(tm + d, nt)},
            device_id_type=MESH,
        )
        copy.start()
        copies.append(copy)
    own.wait()
    for copy in copies:
        copy.wait()
    all_ref[...] = buf[...]


def states(st, nt):
    vmem = pl.BlockSpec(memory_space=pltpu.VMEM)
    dma = pltpu.SemaphoreType.DMA
    return pl.pallas_call(
        functools.partial(states_kernel, nt),
        out_shape=jax.ShapeDtypeStruct((nt,) + st.shape, F32),
        in_specs=[vmem],
        out_specs=vmem,
        scratch_shapes=[pltpu.VMEM((nt,) + st.shape, F32), dma, dma((nt,)), dma((nt,))],
        compiler_params=pltpu.CompilerParams(collective_id=1, has_side_effects=True),
        name="states",
    )(st)


def final_kernel(
    nt, w_ref, yx_ref, zx_ref, all_ref, rate_ref, gaps_ref, o_ref,
    back_ref, halved_ref, sp_ref, g_ref, product_ref, level_ref,
):
    tm = lax.axis_index("tm")

    @pl.when(pl.program_id(0) == 0)
    def _():
        back_ref[...] = permutation(True).astype(BF16)
        halved = halvings(gaps_ref)
        halved_ref[...] = halved
        sp_ref[...] = own_halvings(halved_ref, permutation(False))
        by = 1
        while by < 128:
            halved = halved * pltpu.roll(halved, by, axis=1)
            by *= 2
        product_ref[...] = halved
        seg = lax.broadcasted_iota(jnp.int32, (SEGS, BLK), 0)
        g = jnp.where(seg >= 1, shifted(seg_product(sp_ref), 1), 1.0)
        by = 1
        while by < SEGS:
            g = g * jnp.where(seg >= by, shifted(g, by), 1.0)
            by *= 2
        g_ref[...] = g

    rate = rate_ref[...]
    block_decay = jnp.exp(-(float(BLK) * rate))
    y = jnp.zeros((1, BLK), F32)
    z = jnp.zeros((1, BLK), F32)
    for b in range(nt - 1):
        slot = lax.rem(tm - b + nt, nt)
        product = product_ref[2 * b : 2 * b + 1, :] * product_ref[2 * b + 1 : 2 * b + 2, :]
        f = block_decay * jnp.concatenate([product, product], axis=1)
        here = b < tm
        znew = f * (z + float(BLK) * y) + all_ref[slot, 1:2, :]
        ynew = f * y + all_ref[slot, 0:1, :]
        z = jnp.where(here, znew, z)
        y = jnp.where(here, ynew, y)

    seg = lax.broadcasted_iota(jnp.int32, (SEGS, BLK), 0)
    ahead = (seg * (BLK // SEGS)).astype(F32)
    f = g_ref[...] * jnp.exp(-(ahead * rate))
    z = zx_ref[...] + f * (z + ahead * y)
    y = yx_ref[...] + f * y
    e = jnp.broadcast_to(jnp.exp(-rate), (SEGS, BLK))
    gain = jnp.broadcast_to(2.0 * rate * jnp.sqrt(rate), (SEGS, BLK))
    for k in range(BLK // SEGS):
        a = e * sp_ref[SEGS * k : SEGS * (k + 1), :]
        z = a * (z + y)
        y = a * y + w_ref[SEGS * k : SEGS * (k + 1), :]
        level_ref[SEGS * k : SEGS * (k + 1), :] = gain * z
    o_ref[...] = dot(back_ref[...], level_ref[...].astype(BF16)).astype(BF16)


def final(w, yx, zx, everyone, rates, gaps):
    time_rows, stations = w.shape
    nt = everyone.shape[0]
    tile = pl.BlockSpec((time_rows, BLK), lambda i: (0, i))
    line = pl.BlockSpec((SEGS, BLK), lambda i: (0, i))
    return pl.pallas_call(
        functools.partial(final_kernel, nt),
        grid=(stations // BLK,),
        out_shape=jax.ShapeDtypeStruct((time_rows, stations), BF16),
        in_specs=[
            tile,
            line,
            line,
            pl.BlockSpec((nt, 2, BLK), lambda i: (0, 0, i)),
            pl.BlockSpec((1, BLK), lambda i: (0, i)),
            pl.BlockSpec(gaps.shape, lambda i: (0, 0)),
        ],
        out_specs=tile,
        scratch_shapes=[
            pltpu.VMEM((BLK, BLK), BF16),
            pltpu.VMEM(gaps.shape, F32),
            pltpu.VMEM((BLK, BLK), F32),
            pltpu.VMEM((SEGS, BLK), F32),
            pltpu.VMEM(gaps.shape, F32),
            pltpu.VMEM((BLK, BLK), F32),
        ],
        name="final",
    )(w, yx, zx, everyone, rates, gaps)


def on_device(nx, nz, nt, right_sides, factor_cols, diag_inverses, panel_block, decay_rate, gaps):
    stations = right_sides.shape[1]
    rates = decay_rate.reshape(1, stations)
    gaps = gaps.reshape(-1, 128)
    candidates = pick(right_sides, factor_cols, panel_block, nx)
    panel, f10 = spread(candidates, panel_block, nx, nz, stations // BLK)
    w, yx, zx, st = local(
        panel, f10, diag_inverses, right_sides, factor_cols, rates, gaps, panel_block
    )
    return final(w, yx, zx, states(st, nt), rates, gaps)


def solution(mesh):
    nz = RING
    nx = mesh.shape["stn"] // nz
    return jax.shard_map(
        functools.partial(on_device, nx, nz, mesh.shape["tm"]),
        mesh=mesh,
        in_specs=(P("tm", "stn"), P("stn", None), P(), P(), P("stn"), P()),
        out_specs=P("tm", "stn"),
        check_vma=False,
    )
```

time: 695 us -> 81.7 us (0.12)
  waiting for transfers between devices: 547 us -> 0 us
  Pallas kernels: 0 us -> 80.5 us
  local copies, waits for them, and re-layouts: 42 us -> 0 us
  other arithmetic: 31.4 us -> 0 us
  blocking collectives: 19.4 us -> 0 us
  starting transfers between devices: 15.1 us -> 0 us
  loops' own time: 14.9 us -> 0 us
  between operations: 14.2 us -> 0.67 us
  matrix products: 10.7 us -> 0 us
    psum x2 -> x0, waiting for transfers between devices: 521 us -> none  [broadcast(): return lax.psum(block, axis)]
    pallas_call x0 -> x5, Pallas kernels: none -> 80.5 us  [the longest x1 53.5 us: spread(): pl.pallas_call(functools.partial(spread_kernel, nx, nz, blocks), out_shap...]
    slice x1224 -> x0, local copies, waits for them, and re-layouts: 29.4 us -> none  [the longest x1216 29.4 us: block_prefix(): return lax.associative_scan(compose, elements, axis=0)]
    all_to_all x1 -> x0, waiting for transfers between devices: 25.5 us -> none  [on_device(): series = lax.all_to_all(work, 'tm', split_axis=1, concat_axis=0, tiled=True)]
    all_to_all x1 -> x0, blocking collectives: 19.4 us -> none  [on_device(): return lax.all_to_all(levels, 'tm', split_axis=0, concat_axis=1, tiled=True)]
    add x544 -> x0, other arithmetic: 17.8 us -> none  [the longest x8 9.08 us: block_prefix(): factor * (-decay * rate * rate) + 0.0 * inputs]
    all_to_all x1 -> x0, starting transfers between devices: 15.1 us -> none  [on_device(): series = lax.all_to_all(work, 'tm', split_axis=1, concat_axis=0, tiled=True)]
    another operation x1 -> x0, loops' own time: 14.9 us -> none  [on_device(): lax.scan(advance, (zeros_row, zeros_row), (series_blocks, gap_blocks))]
  transfers between devices with their start and end apart: 3 -> 0, of which waited for: 3 -> 0; matrix products, arithmetic and copies ran while one was open for 1% -> 0% of each run, Pallas kernels for 0% -> 0%
where the time goes in v1:
time: 81.7 us; the launch traced here: 81.2 us
  Pallas kernels  80.5 us (99%)
    pallas_call x1, Pallas kernels, spread(): pl.pallas_call(functools.partial(spread_kernel, nx, nz, blocks), out_shap...  53.5 us
    pallas_call x1, Pallas kernels, local(): pl.pallas_call(local_kernel, grid=(stations // BLK,), out_shape=(jax.Shap...  9.38 us
    pallas_call x1, Pallas kernels, states(): pl.pallas_call(functools.partial(states_kernel, nt), out_shape=jax.ShapeD...  8.86 us
    pallas_call x1, Pallas kernels, final(): pl.pallas_call(functools.partial(final_kernel, nt), grid=(stations // BLK...  7.03 us
    pallas_call x1, Pallas kernels, pick(): pl.pallas_call(functools.partial(pick_kernel, nx), out_shape=jax.ShapeDty...  1.79 us

profile of v1, /device:TPU:1, one launch (start us, length us, event | category | flops | bytes accessed | tf_op | source)
XLA Modules:
  0.0 81.2 jit_solution(2678461066375975567)
XLA Ops:
  0.7 1.8 %pick.1.c_ref = bf16[4,80,512]{2,1,0:T(8,128)(2,1)} custom-call(s32[1]{0:T(128)S(6)} %copy.7.pb_ref, bf16[256,2048]{1,0:T(8,128)(2,1)} %r_ref.1, bf16[256,2048]{1,0:T(8,128)(2,1)} %r_ref.1, bf16[2048,512]{1,0:T(8,128)(2,1)} %fc_ref.1), custom_call_target="tpu_custom_call" | custom-call | tf_op jit(solution)/shard_map/pick/pallas_call | solution.py:51
  2.4 53.5 %spread.1 = (bf16[256,512]{1,0:T(8,128)(2,1)}, bf16[128,512]{1,0:T(8,128)(2,1)}) custom-call(s32[1]{0:T(128)S(6)} %copy.7.pb_ref, bf16[4,80,512]{2,1,0:T(8,128)(2,1)} %pick.1.c_ref), custom_call_target="tpu_custom_call" | custom-call | tf_op jit(solution)/shard_map/spread/pallas_call | solution.py:220
  55.9 9.4 %local.1 = (f32[256,2048]{1,0:T(8,128)}, f32[8,2048]{1,0:T(8,128)}, f32[8,2048]{1,0:T(8,128)}, f32[2,2048]{1,0:T(2,128)}) custom-call(s32[1]{0:T(128)S(6)} %copy.7.pb_ref, bf16[256,512]{1,0:T(8,128)(2,1)} %get-tuple-element.11.panel_ref, bf16[128,512]{1,0:T(8,128)(2,1)} %get-tuple-element.12.f10_ref, f32[2,256,256]{2,1,0:T(8,128)} %diag_ref.1, ...), custom_call_target="tpu_custom_call" | custom-call | tf_op jit(solution)/shard_map/local/pallas_call | solution.py:363
  65.3 8.9 %states.1.all_ref = f32[8,2,2048]{2,1,0:T(2,128)} custom-call(f32[2,2048]{1,0:T(2,128)} %get-tuple-element.16.st_ref), custom_call_target="tpu_custom_call" | custom-call | tf_op jit(solution)/shard_map/states/pallas_call | solution.py:426
  74.2 7.0 %final.1 = bf16[256,2048]{1,0:T(8,128)(2,1)} custom-call(f32[256,2048]{1,0:T(8,128)} %get-tuple-element.13.w_ref, f32[8,2048]{1,0:T(8,128)} %get-tuple-element.14.yx_ref, f32[8,2048]{1,0:T(8,128)} %get-tuple-element.15.zx_ref, f32[8,2,2048]{2,1,0:T(2,128)} %states.1.all_ref, f32[1,2048]{1,0:T(1,128)} %bitcast.3, s32[16,128]{1,0:T(8,128)} %bitcast.5), custom_call_target="tpu_custom_call" | custom-call | tf_op jit(solution)/shard_map/final/pallas_call | solution.py:496
